TPU v7x, 32 devices: a whole 2x2x4 slice. The times are simulated.
32 devices in a mesh: src: 2 (over x), tgt: 16 (over z, y, core).
Axes of the slice: x: 2, y: 2, z: 4, core: 2. Of those that a mesh axis runs over, the one named last changes fastest.
Arguments:
- src_emb: bfloat16 [8192, 256], P(('src', 'tgt')), may hold values from -32 to 32
- tgt_emb: bfloat16 [16384, 256], P(('tgt', 'src')), may hold values from -32 to 32
- block_rows: int32 [2, 16, 24], P('src', 'tgt'), may hold values from 0 to 15, as said below
- block_cols: int32 [2, 16, 24], P('src', 'tgt'), may hold values from 0 to 3
- block_counts: int32 [2, 16], P('src', 'tgt'), may hold values from 4 to 24, as said below
Outputs:
- transport: bfloat16 [2, 16, 24, 256, 256], P('src', 'tgt')
- row_potential: float32 [8192], P(('src', 'tgt'))
- col_potential: float32 [16384], P(('tgt', 'src'))
Inputs may be any that keep to these rules, and one draw needn't show every extreme that they name: The 24 slots of one device name distinct blocks (block_rows, block_cols); its first 4 slots name every local block column once; every local block row of a src index is named by a live slot of some device of that index. `block_counts`: exactly 24 on some device.
All inputs are finite; a program needn't handle non-finite values.
Results may differ from a plain program's by a relative error of at most 0.0019.
The roundings to bfloat16 on the way count: a program that leaves them out, or rounds other values in their place, can miss the bound.
Values may be sent and summed in bfloat16 or wider, within the bound.
No kernel may reach another device: no remote copies, remote signals or barrier semaphores. Data moves between devices by JAX's collectives and lax.ppermute only.
A program may use at most 64 MiB of HBM per device.

v0:
```python
import math
import jax
import jax.numpy as jnp
from jax import lax
from jax.sharding import PartitionSpec as P

DIM = 256
BLOCK = 256
ROW_BLOCKS = 16
COL_BLOCKS = 4
SLOTS = 24
ITERS = 3
inv_temp = 250.0
sentinel = -1e30
highest = lax.Precision.HIGHEST


def unit_rows(embedding):
    values = embedding.astype(jnp.float32)
    inverse_norm = lax.rsqrt(jnp.sum(values * values, axis=1, keepdims=True) + 1e-06)
    return (values * inverse_norm).astype(jnp.bfloat16)


def spread_top(slot_top, slot_hot):
    return jnp.max(jnp.where(slot_hot[:, :, None] > 0, slot_top[:, None, :], sentinel), axis=0)


def spread_sum(slot_sums, slot_hot):
    return jnp.einsum("cn,cb->nb", slot_hot, slot_sums, precision=highest)


def row_potential(scores, col_slots, rows_idx, row_hot):
    shifted = scores + col_slots[:, None, :]
    top_local = spread_top(jnp.max(shifted, axis=2), row_hot)
    top_value = lax.pmax(top_local, "tgt")
    slot_sums = jnp.sum(jnp.exp(shifted - top_value[rows_idx][:, :, None]), axis=2)
    sum_total = lax.psum(spread_sum(slot_sums, row_hot), "tgt")
    row_dual = -(top_value + jnp.log(sum_total))
    share_width = row_dual.size // lax.axis_size("tgt")
    own_rows = lax.dynamic_slice_in_dim(
        row_dual.reshape(-1), lax.axis_index("tgt") * share_width, share_width
    )
    return (row_dual, own_rows)


def col_potential(scores, row_slots, cols_idx, col_hot, log_ratio):
    shifted = scores + row_slots[:, :, None]
    top_local = spread_top(jnp.max(shifted, axis=1), col_hot)
    top_value = lax.pmax(top_local, "src")
    slot_sums = jnp.sum(jnp.exp(shifted - top_value[cols_idx][:, None, :]), axis=1)
    sum_total = lax.psum(spread_sum(slot_sums, col_hot), "src")
    return log_ratio - (top_value + jnp.log(sum_total))


def shards(src_emb, tgt_emb, block_rows, block_cols, block_counts):
    src_rows = lax.all_gather(unit_rows(src_emb), "tgt", axis=0, tiled=True)
    tgt_rows = lax.all_gather(unit_rows(tgt_emb), "src", axis=0, tiled=True)
    rows_idx = block_rows[0, 0]
    cols_idx = block_cols[0, 0]
    live_slot = jnp.arange(SLOTS, dtype=jnp.int32) < block_counts[0, 0]
    row_hot = (
        (rows_idx[:, None] == jnp.arange(ROW_BLOCKS, dtype=jnp.int32)[None, :]) & live_slot[:, None]
    ).astype(jnp.float32)
    col_hot = (
        (cols_idx[:, None] == jnp.arange(COL_BLOCKS, dtype=jnp.int32)[None, :]) & live_slot[:, None]
    ).astype(jnp.float32)
    src_blocks = src_rows.reshape(ROW_BLOCKS, BLOCK, DIM)[rows_idx]
    tgt_blocks = tgt_rows.reshape(COL_BLOCKS, BLOCK, DIM)[cols_idx]
    products = jnp.einsum(
        "cbe,cde->cbd", src_blocks, tgt_blocks, preferred_element_type=jnp.float32
    )
    scores = jnp.where(live_slot[:, None, None], products * inv_temp, sentinel)
    log_ratio = math.log(ROW_BLOCKS * lax.axis_size("src") / (COL_BLOCKS * lax.axis_size("tgt")))
    col_dual = jnp.zeros((COL_BLOCKS, BLOCK), jnp.float32)
    row_dual = jnp.zeros((ROW_BLOCKS, BLOCK), jnp.float32)
    own_rows = jnp.zeros((ROW_BLOCKS * BLOCK // lax.axis_size("tgt"),), jnp.float32)
    for sweep in range(ITERS):
        row_dual, own_rows = row_potential(scores, col_dual[cols_idx], rows_idx, row_hot)
        col_dual = col_potential(scores, row_dual[rows_idx], cols_idx, col_hot, log_ratio)
    transport = jnp.exp(
        scores + row_dual[rows_idx][:, :, None] + col_dual[cols_idx][:, None, :]
    ).astype(jnp.bfloat16)
    share_width = col_dual.size // lax.axis_size("src")
    own_cols = lax.dynamic_slice_in_dim(
        col_dual.reshape(-1), lax.axis_index("src") * share_width, share_width
    )
    return (transport[None, None], own_rows / inv_temp, own_cols / inv_temp)


def solution(mesh):
    return jax.shard_map(
        shards,
        mesh=mesh,
        in_specs=(
            P(("src", "tgt"), None),
            P(("tgt", "src"), None),
            P("src", "tgt", None),
            P("src", "tgt", None),
            P("src", "tgt"),
        ),
        out_specs=(P("src", "tgt", None, None, None), P(("src", "tgt")), P(("tgt", "src"))),
        check_vma=False,
    )
```

profile of v0, /device:TPU:0, one launch (start us, length us, event | category | flops | bytes accessed | tf_op | source)
XLA Modules:
  0.0 503.7 jit_solution(15820733972963911582)
XLA Ops:
  7.2 0.0 all-gather.2.cloned.1.call-start
  7.2 1.0 fusion.3
  8.3 1.7 fusion.4
  9.9 0.0 all-gather.2.cloned.1.call-update
  10.0 0.7 fusion.20
  10.6 0.6 gather_fusion.2
  11.2 1.1 fusion.1
  12.3 1.1 fusion.2
  13.4 9.9 %all_gather.7 = bf16[1024,256]{1,0:T(8,128)(2,1)S(1)} all-gather(bf16[512,256]{1,0:T(8,128)(2,1)S(1)} %fusion.2), channel_id=1, replica_groups=mesh['src'=2,'tgt'=16] {'src'}, dimensions={0}, use_global_device_ids=true | all-gather | bytes 786432 | tf_op jit(solution)/shard_map/all_gather | solution.py:57
  23.4 2.5 gather_fusion.1
  26.8 0.1 convert_compare_fusion
  26.8 28.1 %all-gather.2.cloned.1.call-done = bf16[4096,256]{1,0:T(8,128)(2,1)} async-done(((bf16[256,256]{1,0:T(8,128)(2,1)}), bf16[4096,256]{1,0:T(8,128)(2,1)}) %all-gather.2.cloned.1.call-update) | async-done | bytes 2097168 | tf_op jit(solution)/shard_map/all_gather | solution.py:56
  54.9 4.1 gather_fusion
  59.0 5.9 %add_reduce_fusion.4 = (f32[24,256]{1,0:T(8,128)S(1)}, f32[24,256,256]{2,1,0:T(8,128)}) fusion(f32[24,256]{1,0:T(8,128)S(1)} %gather_fusion.2, bf16[24,256,256]{2,1,0:T(8,128)(2,1)} %gather_fusion, bf16[24,256,256]{2,1,0:T(8,128)(2,1)S(1)} %copy-done, pred[24]{0:T(512)(128)(4,1)S(1)} %iota_compare_fusion.2), kind=kOutput, calls=%fused_computation.27 | convolution fusion | flops 811591680 | bytes 12632088 | tf_op jit(solution)/shard_map/cbe,cde->cbd/dot_general | solution.py:69
  64.9 0.1 select_reduce_fusion.2
  65.0 59.4 %pmax.42 = f32[16,256]{1,0:T(8,128)S(1)} all-reduce(f32[16,256]{1,0:T(8,128)S(1)} %select_reduce_fusion.2), channel_id=1, replica_groups=mesh['src'=2,'tgt'=16] {'tgt'}, use_global_device_ids=true, to_apply=%region_4.5 | all-reduce | flops 4096 | bytes 32768 | tf_op jit(solution)/shard_map/pmax | solution.py:35
  124.4 0.6 gather_fusion.3
  125.0 3.9 exponential_reduce_fusion.5
  128.9 0.3 fusion.10
  129.2 57.6 %psum.42 = f32[16,256]{1,0:T(8,128)S(1)} all-reduce(f32[16,256]{1,0:T(8,128)S(1)} %fusion.10), channel_id=1, replica_groups=mesh['src'=2,'tgt'=16] {'tgt'}, use_global_device_ids=true, to_apply=%region_6.7 | all-reduce | flops 4096 | bytes 32768 | tf_op jit(solution)/shard_map/psum | solution.py:37
  186.8 0.6 gather_fusion.4
  187.4 3.4 add_reduce_fusion.3
  190.8 0.1 select_reduce_fusion.5
  190.9 4.9 pmax.43
  195.8 0.6 gather_fusion.5
  196.4 3.6 exponential_reduce_fusion.4
  199.9 0.1 fusion.22
  200.1 4.9 psum.43
  205.0 0.6 gather_fusion.6
  205.6 3.7 add_reduce_fusion.2
  209.3 0.1 select_reduce_fusion.1
  209.4 57.6 %pmax.44 = f32[16,256]{1,0:T(8,128)S(1)} all-reduce(f32[16,256]{1,0:T(8,128)S(1)} %select_reduce_fusion.1), channel_id=1, replica_groups=mesh['src'=2,'tgt'=16] {'tgt'}, use_global_device_ids=true, to_apply=%region_14.15 | all-reduce | flops 4096 | bytes 32768 | tf_op jit(solution)/shard_map/pmax | solution.py:35
  267.0 0.6 gather_fusion.7
  267.6 3.9 exponential_reduce_fusion.3
  271.5 0.3 fusion.8
  271.7 57.6 %psum.44 = f32[16,256]{1,0:T(8,128)S(1)} all-reduce(f32[16,256]{1,0:T(8,128)S(1)} %fusion.8), channel_id=1, replica_groups=mesh['src'=2,'tgt'=16] {'tgt'}, use_global_device_ids=true, to_apply=%region_16.17 | all-reduce | flops 4096 | bytes 32768 | tf_op jit(solution)/shard_map/psum | solution.py:37
  329.4 0.6 gather_fusion.8
  330.0 3.4 add_reduce_fusion.1
  333.3 0.1 select_reduce_fusion.4
  333.4 4.9 pmax.45
  338.4 0.6 gather_fusion.9
  339.0 3.6 exponential_reduce_fusion.2
  342.5 0.1 fusion.23
  342.6 4.9 psum.45
  347.6 0.6 gather_fusion.10
  348.2 3.7 add_reduce_fusion
  351.9 0.1 select_reduce_fusion
  352.0 57.8 %pmax.46 = f32[16,256]{1,0:T(8,128)S(1)} all-reduce(f32[16,256]{1,0:T(8,128)S(1)} %select_reduce_fusion), channel_id=1, replica_groups=mesh['src'=2,'tgt'=16] {'tgt'}, use_global_device_ids=true, to_apply=%region_24.25 | all-reduce | flops 4096 | bytes 32768 | tf_op jit(solution)/shard_map/pmax | solution.py:35
  409.8 0.6 gather_fusion.11
  410.4 3.9 exponential_reduce_fusion.1
  414.2 0.3 fusion.6
  414.5 57.6 %psum.46 = f32[16,256]{1,0:T(8,128)S(1)} all-reduce(f32[16,256]{1,0:T(8,128)S(1)} %fusion.6), channel_id=1, replica_groups=mesh['src'=2,'tgt'=16] {'tgt'}, use_global_device_ids=true, to_apply=%region_26.27 | all-reduce | flops 4096 | bytes 32768 | tf_op jit(solution)/shard_map/psum | solution.py:37
  472.1 0.6 gather_fusion.12
  472.7 3.4 add_reduce_fusion.5
  476.1 0.1 select_reduce_fusion.3
  476.2 4.9 pmax.47
  481.1 0.6 gather_fusion.13
  481.7 3.6 exponential_reduce_fusion
  485.3 0.1 fusion.24
  485.4 4.9 psum.47
  490.3 0.6 gather_fusion.14
  490.9 4.6 fusion
  495.5 0.7 dynamic-slice_multiply_fusion
  496.2 0.6 dynamic-slice_multiply_fusion.1
  (22 shorter events, 0.1 us)
Async XLA Ops:
  7.2 19.6 %copy-start.1 = (s32[1,1,24]{2,1,0:T(1,128)S(1)}, s32[1,1,24]{2,1,0:T(1,128)}, u32[]{:S(2)}) copy-start(s32[1,1,24]{2,1,0:T(1,128)} %param.8) | copy-start | bytes 292
  7.2 19.5 %copy-start.2 = (s32[1,1,24]{2,1,0:T(1,128)S(1)}, s32[1,1,24]{2,1,0:T(1,128)}, u32[]{:S(2)}) copy-start(s32[1,1,24]{2,1,0:T(1,128)} %param.7) | copy-start | bytes 292
  7.2 47.8 %all-gather.2.cloned.1.call-start = ((), (), s32[]{:S(2)}) async-start(), calls=%async_computation | async-start | bytes 2228224 | tf_op jit(solution)/shard_map/all_gather | solution.py:56
  25.9 33.2 %copy-start = (bf16[24,256,256]{2,1,0:T(8,128)(2,1)S(1)}, bf16[24,256,256]{2,1,0:T(8,128)(2,1)}, u32[]{:S(2)}) copy-start(bf16[24,256,256]{2,1,0:T(8,128)(2,1)} %gather_fusion.1) | copy-start | bytes 9437188
Sparse Core Ops, SparseCore 0:
  10.7 44.1 all-gather.1
where the time goes:
time: 504 us
  blocking collectives  387 us (77%)
  other arithmetic  51.9 us (10%)
  waiting for transfers between devices  28.1 us (6%)
  between operations  15.1 us (3%)
  local copies, waits for them, and re-layouts  14.3 us (3%)
  matrix products  7.02 us (1%)
    pmax x3, blocking collectives, row_potential(): top_value = lax.pmax(top_local, 'tgt')  175 us
    psum x3, blocking collectives, row_potential(): sum_total = lax.psum(spread_sum(slot_sums, row_hot), 'tgt')  173 us
    all_gather x1, waiting for transfers between devices, shards(): src_rows = lax.all_gather(unit_rows(src_emb), 'tgt', axis=0, tiled=True)  28.1 us
    pmax x3, blocking collectives, col_potential(): top_value = lax.pmax(top_local, 'src')  14.8 us
    psum x3, blocking collectives, col_potential(): sum_total = lax.psum(spread_sum(slot_sums, col_hot), 'src')  14.8 us
    reduce_sum x3, other arithmetic, row_potential(): jnp.sum(jnp.exp(shifted - top_value[rows_idx][:, :, None]), axis=2)  11.6 us
    reduce_sum x3, other arithmetic, col_potential(): jnp.sum(jnp.exp(shifted - top_value[cols_idx][:, None, :]), axis=1)  10.7 us
    reduce_max x3, other arithmetic, col_potential(): top_local = spread_top(jnp.max(shifted, axis=1), col_hot)  10.1 us
  transfers between devices with their start and end apart: 1, of which 1 were waited for; matrix products, arithmetic and copies ran while one was open for 1% of the time, Pallas kernels for 0%

commit v1 on v0

--- a/solution.py
+++ b/solution.py
@@ -34,7 +34,7 @@
     top_local = spread_top(jnp.max(shifted, axis=2), row_hot)
     top_value = lax.pmax(top_local, "tgt")
     slot_sums = jnp.sum(jnp.exp(shifted - top_value[rows_idx][:, :, None]), axis=2)
-    sum_total = lax.psum(spread_sum(slot_sums, row_hot), "tgt")
+    sum_total = jnp.sum(lax.all_gather(spread_sum(slot_sums, row_hot), "tgt"), axis=0)
     row_dual = -(top_value + jnp.log(sum_total))
     share_width = row_dual.size // lax.axis_size("tgt")
     own_rows = lax.dynamic_slice_in_dim(

time: 504 us -> 385 us (0.76)
  blocking collectives: 387 us -> 268 us
    psum x3 -> x0, blocking collectives: 173 us -> none  [row_potential(): sum_total = lax.psum(spread_sum(slot_sums, row_hot), 'tgt')]
    all_gather x0 -> x3, blocking collectives: none -> 53.5 us  [row_potential(): lax.all_gather(spread_sum(slot_sums, row_hot), 'tgt')]
  transfers between devices with their start and end apart: 1 -> 1, of which waited for: 1 -> 1; matrix products, arithmetic and copies ran while one was open for 1% -> 2% of each run, Pallas kernels for 0% -> 0%
where the time goes in v1:
time: 385 us; the launch traced here: 384 us
  blocking collectives  268 us (70%)
  other arithmetic  52 us (14%)
  waiting for transfers between devices  28.1 us (7%)
  between operations  15.1 us (4%)
  local copies, waits for them, and re-layouts  14.3 us (4%)
  matrix products  7.02 us (2%)
    pmax x3, blocking collectives, row_potential(): top_value = lax.pmax(top_local, 'tgt')  175 us
    all_gather x3, blocking collectives, row_potential(): lax.all_gather(spread_sum(slot_sums, row_hot), 'tgt')  53.5 us
    all_gather x1, waiting for transfers between devices, shards(): src_rows = lax.all_gather(unit_rows(src_emb), 'tgt', axis=0, tiled=True)  28.1 us
    pmax x3, blocking collectives, col_potential(): top_value = lax.pmax(top_local, 'src')  14.8 us
    psum x3, blocking collectives, col_potential(): sum_total = lax.psum(spread_sum(slot_sums, col_hot), 'src')  14.8 us
    reduce_sum x3, other arithmetic, row_potential(): jnp.sum(jnp.exp(shifted - top_value[rows_idx][:, :, None]), axis=2)  11.6 us
    reduce_sum x3, other arithmetic, col_potential(): jnp.sum(jnp.exp(shifted - top_value[cols_idx][:, None, :]), axis=1)  10.7 us
    reduce_max x3, other arithmetic, col_potential(): top_local = spread_top(jnp.max(shifted, axis=1), col_hot)  10.1 us
  transfers between devices with their start and end apart: 1, of which 1 were waited for; matrix products, arithmetic and copies ran while one was open for 2% of the time, Pallas kernels for 0%

profile of v1, /device:TPU:0, one launch (start us, length us, event | category | flops | bytes accessed | tf_op | source)
XLA Modules:
  0.0 384.4 jit_solution(148279379508810752)
XLA Ops:
  7.2 0.0 all-gather.5.cloned.1.call-start
  7.2 1.0 fusion.3
  8.3 1.7 fusion.4
  9.9 0.0 all-gather.5.cloned.1.call-update
  10.0 0.7 fusion.20
  10.6 0.6 gather_fusion.2
  11.2 1.1 fusion.1
  12.3 1.1 fusion.2
  13.4 9.9 %all_gather.25 = bf16[1024,256]{1,0:T(8,128)(2,1)S(1)} all-gather(bf16[512,256]{1,0:T(8,128)(2,1)S(1)} %fusion.2), channel_id=1, replica_groups=mesh['src'=2,'tgt'=16] {'src'}, dimensions={0}, use_global_device_ids=true | all-gather | bytes 786432 | tf_op jit(solution)/shard_map/all_gather | solution.py:57
  23.4 2.5 gather_fusion.1
  26.8 0.1 convert_compare_fusion
  26.8 28.1 %all-gather.5.cloned.1.call-done = bf16[4096,256]{1,0:T(8,128)(2,1)} async-done(((bf16[256,256]{1,0:T(8,128)(2,1)}), bf16[4096,256]{1,0:T(8,128)(2,1)}) %all-gather.5.cloned.1.call-update) | async-done | bytes 2097168 | tf_op jit(solution)/shard_map/all_gather | solution.py:56
  54.9 4.1 %gather_fusion = bf16[24,256,256]{2,1,0:T(8,128)(2,1)} fusion(bf16[16,256,256]{2,1,0:T(8,128)(2,1)} %bitcast.36, s32[1024]{0:T(1024)S(1)} %pad_clamp_fusion.1), kind=kCustom, calls=%fused_computation | custom fusion | bytes 6291552 | tf_op jit(solution)/shard_map/gather | solution.py:67
  59.0 5.9 %add_reduce_fusion.4 = (f32[24,256]{1,0:T(8,128)S(1)}, f32[24,256,256]{2,1,0:T(8,128)}) fusion(f32[24,256]{1,0:T(8,128)S(1)} %gather_fusion.2, bf16[24,256,256]{2,1,0:T(8,128)(2,1)} %gather_fusion, bf16[24,256,256]{2,1,0:T(8,128)(2,1)S(1)} %copy-done, pred[24]{0:T(512)(128)(4,1)S(1)} %iota_compare_fusion.2), kind=kOutput, calls=%fused_computation.27 | convolution fusion | flops 811591680 | bytes 12632088 | tf_op jit(solution)/shard_map/cbe,cde->cbd/dot_general | solution.py:69
  64.9 0.1 select_reduce_fusion.2
  65.0 59.4 %pmax.42 = f32[16,256]{1,0:T(8,128)S(1)} all-reduce(f32[16,256]{1,0:T(8,128)S(1)} %select_reduce_fusion.2), channel_id=1, replica_groups=mesh['src'=2,'tgt'=16] {'tgt'}, use_global_device_ids=true, to_apply=%region_4.5 | all-reduce | flops 4096 | bytes 32768 | tf_op jit(solution)/shard_map/pmax | solution.py:35
  124.4 0.6 gather_fusion.3
  125.0 3.9 %exponential_reduce_fusion.5 = f32[24,256]{1,0:T(8,128)S(1)} fusion(f32[24,256,256]{2,1,0:T(8,128)} %get-tuple-element.6, f32[24,256]{1,0:T(8,128)S(1)} %gather_fusion.3, f32[24,256]{1,0:T(8,128)S(1)} %gather_fusion.2), kind=kLoop, calls=%fused_computation.21 | loop fusion | flops 4712448 | bytes 6365184 | tf_op jit(solution)/shard_map/reduce_sum | solution.py:36
  128.9 0.3 fusion.10
  129.2 17.8 %all-gather = f32[256,256]{1,0:T(8,128)S(1)} all-gather(f32[16,256]{1,0:T(8,128)S(1)} %fusion.10), channel_id=2, replica_groups=mesh['src'=2,'tgt'=16] {'tgt'}, dimensions={0}, use_global_device_ids=true | all-gather | bytes 278528 | tf_op jit(solution)/shard_map/all_gather | solution.py:37
  147.0 0.6 gather_fusion.4
  147.6 3.4 add_reduce_fusion.3
  151.0 0.1 select_reduce_fusion.5
  151.1 4.9 %pmax.43 = f32[4,256]{1,0:T(4,128)S(1)} all-reduce(f32[4,256]{1,0:T(4,128)S(1)} %select_reduce_fusion.5), channel_id=1, replica_groups=mesh['src'=2,'tgt'=16] {'src'}, use_global_device_ids=true, to_apply=%region_9.10 | all-reduce | flops 1024 | bytes 8192 | tf_op jit(solution)/shard_map/pmax | solution.py:49
  156.0 0.6 gather_fusion.5
  156.6 3.6 exponential_reduce_fusion.4
  160.2 0.1 fusion.22
  160.3 4.9 %psum.21 = f32[4,256]{1,0:T(4,128)S(1)} all-reduce(f32[4,256]{1,0:T(4,128)S(1)} %fusion.22), channel_id=1, replica_groups=mesh['src'=2,'tgt'=16] {'src'}, use_global_device_ids=true, to_apply=%region_11.12 | all-reduce | flops 1024 | bytes 8192 | tf_op jit(solution)/shard_map/psum | solution.py:51
  165.3 0.6 gather_fusion.6
  165.8 3.7 add_reduce_fusion.2
  169.5 0.1 select_reduce_fusion.1
  169.7 57.6 %pmax.44 = f32[16,256]{1,0:T(8,128)S(1)} all-reduce(f32[16,256]{1,0:T(8,128)S(1)} %select_reduce_fusion.1), channel_id=1, replica_groups=mesh['src'=2,'tgt'=16] {'tgt'}, use_global_device_ids=true, to_apply=%region_14.15 | all-reduce | flops 4096 | bytes 32768 | tf_op jit(solution)/shard_map/pmax | solution.py:35
  227.3 0.6 gather_fusion.7
  227.9 3.9 %exponential_reduce_fusion.3 = f32[24,256]{1,0:T(8,128)S(1)} fusion(f32[24,256,256]{2,1,0:T(8,128)} %get-tuple-element.6, f32[24,256]{1,0:T(8,128)S(1)} %gather_fusion.7, f32[24,256]{1,0:T(8,128)S(1)} %gather_fusion.6), kind=kLoop, calls=%fused_computation.19 | loop fusion | flops 4712448 | bytes 6365184 | tf_op jit(solution)/shard_map/reduce_sum | solution.py:36
  231.7 0.3 fusion.8
  232.0 17.8 %all-gather.1 = f32[256,256]{1,0:T(8,128)S(1)} all-gather(f32[16,256]{1,0:T(8,128)S(1)} %fusion.8), channel_id=3, replica_groups=mesh['src'=2,'tgt'=16] {'tgt'}, dimensions={0}, use_global_device_ids=true | all-gather | bytes 278528 | tf_op jit(solution)/shard_map/all_gather | solution.py:37
  249.9 0.6 gather_fusion.8
  250.5 3.4 add_reduce_fusion.1
  253.8 0.1 select_reduce_fusion.4
  253.9 4.9 %pmax.45 = f32[4,256]{1,0:T(4,128)S(1)} all-reduce(f32[4,256]{1,0:T(4,128)S(1)} %select_reduce_fusion.4), channel_id=1, replica_groups=mesh['src'=2,'tgt'=16] {'src'}, use_global_device_ids=true, to_apply=%region_19.20 | all-reduce | flops 1024 | bytes 8192 | tf_op jit(solution)/shard_map/pmax | solution.py:49
  258.9 0.6 gather_fusion.9
  259.5 3.6 exponential_reduce_fusion.2
  263.0 0.1 fusion.23
  263.1 4.9 %psum.22 = f32[4,256]{1,0:T(4,128)S(1)} all-reduce(f32[4,256]{1,0:T(4,128)S(1)} %fusion.23), channel_id=1, replica_groups=mesh['src'=2,'tgt'=16] {'src'}, use_global_device_ids=true, to_apply=%region_21.22 | all-reduce | flops 1024 | bytes 8192 | tf_op jit(solution)/shard_map/psum | solution.py:51
  268.1 0.6 gather_fusion.10
  268.7 3.7 add_reduce_fusion
  272.4 0.1 select_reduce_fusion
  272.5 57.8 %pmax.46 = f32[16,256]{1,0:T(8,128)S(1)} all-reduce(f32[16,256]{1,0:T(8,128)S(1)} %select_reduce_fusion), channel_id=1, replica_groups=mesh['src'=2,'tgt'=16] {'tgt'}, use_global_device_ids=true, to_apply=%region_24.25 | all-reduce | flops 4096 | bytes 32768 | tf_op jit(solution)/shard_map/pmax | solution.py:35
  330.3 0.6 gather_fusion.11
  330.9 3.9 %exponential_reduce_fusion.1 = f32[24,256]{1,0:T(8,128)S(1)} fusion(f32[24,256,256]{2,1,0:T(8,128)} %get-tuple-element.6, f32[24,256]{1,0:T(8,128)S(1)} %gather_fusion.11, f32[24,256]{1,0:T(8,128)S(1)} %gather_fusion.10), kind=kLoop, calls=%fused_computation.17 | loop fusion | flops 4712448 | bytes 6365184 | tf_op jit(solution)/shard_map/reduce_sum | solution.py:36
  334.7 0.3 fusion.6
  335.0 17.8 %all-gather.2 = f32[256,256]{1,0:T(8,128)S(1)} all-gather(f32[16,256]{1,0:T(8,128)S(1)} %fusion.6), channel_id=4, replica_groups=mesh['src'=2,'tgt'=16] {'tgt'}, dimensions={0}, use_global_device_ids=true | all-gather | bytes 278528 | tf_op jit(solution)/shard_map/all_gather | solution.py:37
  352.9 0.6 gather_fusion.12
  353.5 3.4 add_reduce_fusion.5
  356.8 0.1 select_reduce_fusion.3
  356.9 4.9 %pmax.47 = f32[4,256]{1,0:T(4,128)S(1)} all-reduce(f32[4,256]{1,0:T(4,128)S(1)} %select_reduce_fusion.3), channel_id=1, replica_groups=mesh['src'=2,'tgt'=16] {'src'}, use_global_device_ids=true, to_apply=%region_29.30 | all-reduce | flops 1024 | bytes 8192 | tf_op jit(solution)/shard_map/pmax | solution.py:49
  361.9 0.6 gather_fusion.13
  362.5 3.6 exponential_reduce_fusion
  366.0 0.1 fusion.24
  366.2 4.9 %psum.23 = f32[4,256]{1,0:T(4,128)S(1)} all-reduce(f32[4,256]{1,0:T(4,128)S(1)} %fusion.24), channel_id=1, replica_groups=mesh['src'=2,'tgt'=16] {'src'}, use_global_device_ids=true, to_apply=%region_31.32 | all-reduce | flops 1024 | bytes 8192 | tf_op jit(solution)/shard_map/psum | solution.py:51
  371.1 0.6 gather_fusion.14
  371.7 4.6 %fusion = bf16[1,1,24,256,256]{4,3,2,1,0:T(8,128)(2,1)} fusion(f32[24,256,256]{2,1,0:T(8,128)} %get-tuple-element.6, f32[24,256]{1,0:T(8,128)S(1)} %gather_fusion.14, f32[24,256]{1,0:T(8,128)S(1)} %gather_fusion.12), kind=kLoop, calls=%fused_computation.29 | loop fusion | flops 4718592 | bytes 9486336 | tf_op jit(solution)/shard_map/broadcast_in_dim | solution.py:87
  376.3 0.7 dynamic-slice_multiply_fusion
  376.9 0.6 dynamic-slice_multiply_fusion.1
  (25 shorter events, 0.2 us)
Async XLA Ops:
  7.2 19.6 %copy-start.1 = (s32[1,1,24]{2,1,0:T(1,128)S(1)}, s32[1,1,24]{2,1,0:T(1,128)}, u32[]{:S(2)}) copy-start(s32[1,1,24]{2,1,0:T(1,128)} %param.8) | copy-start | bytes 292
  7.2 19.5 %copy-start.2 = (s32[1,1,24]{2,1,0:T(1,128)S(1)}, s32[1,1,24]{2,1,0:T(1,128)}, u32[]{:S(2)}) copy-start(s32[1,1,24]{2,1,0:T(1,128)} %param.7) | copy-start | bytes 292
  7.2 47.8 %all-gather.5.cloned.1.call-start = ((), (), s32[]{:S(2)}) async-start(), calls=%async_computation | async-start | bytes 2228224 | tf_op jit(solution)/shard_map/all_gather | solution.py:56
  25.9 33.2 %copy-start = (bf16[24,256,256]{2,1,0:T(8,128)(2,1)S(1)}, bf16[24,256,256]{2,1,0:T(8,128)(2,1)}, u32[]{:S(2)}) copy-start(bf16[24,256,256]{2,1,0:T(8,128)(2,1)} %gather_fusion.1) | copy-start | bytes 9437188
Sparse Core Ops, SparseCore 0:
  10.7 44.1 all-gather.4
